TPU v7x, 256 devices: a whole 4x4x8 slice. The times are simulated.
256 devices in a mesh: replica: 32 (over y, z_lo, core), fsdp: 8 (over x, z_hi).
Axes of the slice: x: 4, y: 4, z: 8 (z_hi: 2, z_lo: 4; z = z_hi * 4 + z_lo), core: 2. Of those that a mesh axis runs over, the one named last changes fastest.
Arguments:
- tokens: bfloat16 [98304, 8192], P(('replica', 'fsdp')), may hold values from -6 to 6
- inner_weight: bfloat16 [32, 8192, 512], P('replica', 'fsdp'), may hold values from -0.0625 to 0.0625
- cotangent: bfloat16 [98304, 512], P(('replica', 'fsdp')), may hold values from -0.059814453 to 0.059814453
- local_weights: bfloat16 [32, 2, 8192, 896], P('replica', None, 'fsdp'), may hold values from -3 to 3
- anchor: bfloat16 [2, 8, 1024, 896], P(None, 'fsdp', 'replica'), may hold values from -1.5 to 1.5
- momentum: float32 [2, 8, 1024, 896], P(None, 'fsdp', 'replica'), may hold values from -1.5 to 1.5
Outputs:
- keys: bfloat16 [98304, 512], P(('replica', 'fsdp'))
- weight_grad: bfloat16 [32, 8192, 512], P('replica', 'fsdp')
- new_weights: bfloat16 [2, 8192, 896], P(None, 'fsdp')
- new_momentum: float32 [2, 8, 1024, 896], P(None, 'fsdp', 'replica')
All inputs are finite; a program needn't handle non-finite values.
Results may differ from a plain program's by a relative error of at most 0.017.
Values may be sent and summed in bfloat16 or wider, within the bound.
A program may use at most 128 MiB of HBM per device.

v0:
```python
import jax
import jax.numpy as jnp
from jax import lax
from jax.sharding import PartitionSpec as P

outer_rate = 0.7
momentum_decay = 0.9


def outer_step(local_weights, anchor, momentum):
    workers = lax.axis_size("replica")
    local_slab = local_weights[0].astype(jnp.float32)
    summed = lax.psum_scatter(local_slab, "replica", scatter_dimension=1, tiled=True)
    average = summed / workers
    anchor_now = anchor[:, 0].astype(jnp.float32)
    pseudo_grad = anchor_now - average
    momentum_new = momentum_decay * momentum[:, 0] + pseudo_grad
    new_piece = (anchor_now - outer_rate * (pseudo_grad + momentum_decay * momentum_new)).astype(
        jnp.bfloat16
    )
    gathered = lax.all_gather(new_piece, "replica", axis=1, tiled=True)
    return (gathered, momentum_new[:, None])


def inner_pass(tokens, inner_weight, cotangent):
    weight = inner_weight[0]
    columns = tokens
    key_rows = jnp.dot(
        columns,
        lax.all_gather(weight, "fsdp", axis=0, tiled=True),
        preferred_element_type=jnp.float32,
    ).astype(jnp.bfloat16)
    columns = tokens
    grad_sum = lax.psum_scatter(
        lax.dot_general(
            columns, cotangent, (((0,), (0,)), ((), ())), preferred_element_type=jnp.float32
        ).astype(jnp.bfloat16),
        "fsdp",
        scatter_dimension=0,
        tiled=True,
    )
    return (key_rows, grad_sum[None])


def shards(tokens, inner_weight, cotangent, local_weights, anchor, momentum):
    new_weights, new_momentum = outer_step(local_weights, anchor, momentum)
    keys, weight_grad = inner_pass(tokens, inner_weight, cotangent)
    return (keys, weight_grad, new_weights, new_momentum)


def solution(mesh):
    return jax.shard_map(
        shards,
        mesh=mesh,
        in_specs=(
            P(("replica", "fsdp"), None),
            P("replica", "fsdp", None),
            P(("replica", "fsdp"), None),
            P("replica", None, "fsdp", None),
            P(None, "fsdp", "replica", None),
            P(None, "fsdp", "replica", None),
        ),
        out_specs=(
            P(("replica", "fsdp"), None),
            P("replica", "fsdp", None),
            P(None, "fsdp", None),
            P(None, "fsdp", "replica", None),
        ),
        check_vma=False,
    )
```

profile of v0, /device:TPU:32, one launch (start us, length us, event | category | flops | bytes accessed | tf_op | source)
XLA Modules:
  0.0 541.9 jit_solution(11902919102617137104)
XLA Ops:
  8.0 0.0 copy-start
  8.0 0.0 reduce-scatter.5.cloned.1.call-start
  8.1 5.6 %bitcast_convert_fusion = f32[2,1024,896]{2,1,0:T(8,128)} fusion(bf16[1,2,1024,896]{3,2,1,0:T(8,128)(2,1)} %param.9), kind=kLoop, calls=%fused_computation.3 | loop fusion | flops 1835008 | bytes 11010048 | tf_op jit(solution)/shard_map/convert_element_type | solution.py:12
  13.6 0.0 copy-start.1
  13.6 0.0 copy-start.2
  13.6 0.0 reduce-scatter.5.cloned.1.call-update
  13.6 0.0 all-gather.6.cloned.1.call-start
  13.7 0.5 all-gather.6.cloned.1.call-update
  14.2 0.0 all-gather.4.cloned.1.call-start
  14.3 259.8 %reduce-scatter.5.cloned.1.call-done = f32[2,32,896]{2,1,0:T(8,128)} async-done(((f32[2,1024,896]{2,1,0:T(8,128)}), f32[2,32,896]{2,1,0:T(8,128)}) %reduce-scatter.5.cloned.1.call-update) | async-done | bytes 229392 | tf_op jit(solution)/shard_map/reduce_scatter | solution.py:13
  274.1 0.0 copy-done.1
  274.1 0.0 copy-done.2
  274.1 1.7 fusion.6
  275.8 0.0 all-gather.4.cloned.1.call-update
  275.8 0.0 reduce-scatter.3.cloned.1.call-start
  275.9 0.0 copy-done
  275.9 9.6 %convolution_convert_fusion = bf16[8192,512]{1,0:T(8,128)(2,1)} fusion(bf16[384,8192]{1,0:T(8,128)(2,1)} %param.6, bf16[384,512]{1,0:T(8,128)(2,1)S(1)} %copy-done), kind=kOutput, calls=%fused_computation | convolution fusion | flops 3225419776 | bytes 15073280 | tf_op jit(solution)/shard_map/dot_general | solution.py:35
  285.5 0.0 reduce-scatter.3.cloned.1.call-update
  285.5 0.0 all-gather.6.cloned.1.call-done
  285.6 9.4 %fusion.2 = bf16[384,512]{1,0:T(8,128)(2,1)} fusion(bf16[384,8192]{1,0:T(8,128)(2,1)} %param.6, bf16[1,8192,512]{2,1,0:T(8,128)(2,1)} %all-gather.6.cloned.1.call-done), kind=kOutput, calls=%fused_computation.4 | convolution fusion | flops 3221422080 | bytes 15073280 | tf_op jit(solution)/shard_map/dot_general | solution.py:28
  294.9 49.3 %all-gather.4.cloned.1.call-done = bf16[2,1024,896]{2,1,0:T(8,128)(2,1)} async-done(((bf16[2,32,896]{2,1,0:T(8,128)(2,1)}), bf16[2,1024,896]{2,1,0:T(8,128)(2,1)}) %all-gather.4.cloned.1.call-update) | async-done | bytes 3670032 | tf_op jit(solution)/shard_map/all_gather | solution.py:21
  344.2 185.9 %reduce-scatter.3.cloned.1.call-done = bf16[1024,512]{1,0:T(8,128)(2,1)} async-done(((bf16[8192,512]{1,0:T(8,128)(2,1)}), bf16[1024,512]{1,0:T(8,128)(2,1)}) %reduce-scatter.3.cloned.1.call-update) | async-done | bytes 1048592 | tf_op jit(solution)/shard_map/reduce_scatter | solution.py:34
  530.1 4.2 copy.13
Async XLA Ops:
  8.0 267.9 %copy-start = (bf16[384,512]{1,0:T(8,128)(2,1)S(1)}, bf16[384,512]{1,0:T(8,128)(2,1)}, u32[]{:S(2)}) copy-start(bf16[384,512]{1,0:T(8,128)(2,1)} %param.8) | copy-start | bytes 1179652
  8.0 266.0 %reduce-scatter.5.cloned.1.call-start = ((), (), s32[]{:S(2)}) async-start(), calls=%async_computation.3 | async-start | bytes 7569408 | tf_op jit(solution)/shard_map/reduce_scatter | solution.py:13
  13.6 260.4 %copy-start.1 = (f32[2,1,32,896]{3,2,1,0:T(8,128)S(1)}, f32[2,1,32,896]{3,2,1,0:T(8,128)}, u32[]{:S(2)}) copy-start(f32[2,1,32,896]{3,2,1,0:T(8,128)} %param.11) | copy-start | bytes 688132
  13.6 260.4 %copy-start.2 = (bf16[2,1,32,896]{3,2,1,0:T(8,128)(2,1)S(1)}, bf16[2,1,32,896]{3,2,1,0:T(8,128)(2,1)}, u32[]{:S(2)}) copy-start(bf16[2,1,32,896]{3,2,1,0:T(8,128)(2,1)} %param.10) | copy-start | bytes 344068
  13.6 271.9 %all-gather.6.cloned.1.call-start = ((), (), s32[]{:S(2)}) async-start(), calls=%async_computation.5 | async-start | bytes 9437184 | tf_op jit(solution)/shard_map/all_gather | solution.py:30
  14.2 330.0 %all-gather.4.cloned.1.call-start = ((), (), s32[]{:S(2)}) async-start(), calls=%async_computation.4 | async-start | bytes 3784704 | tf_op jit(solution)/shard_map/all_gather | solution.py:21
  275.8 254.3 %reduce-scatter.3.cloned.1.call-start = ((), (), s32[]{:S(2)}) async-start(), calls=%async_computation.2 | async-start | bytes 9437184 | tf_op jit(solution)/shard_map/reduce_scatter | solution.py:34
Sparse Core Ops, SparseCore 0:
  13.8 260.2 reduce-scatter.4
Sparse Core Ops, SparseCore 1:
  16.8 178.4 all-gather.5
  275.9 68.2 all-gather.3
  348.8 181.3 reduce-scatter.2
where the time goes:
time: 542 us
  waiting for transfers between devices  496 us (92%)
  matrix products  19 us (4%)
  between operations  15.7 us (3%)
  other arithmetic  7.29 us (1%)
    reduce_scatter x1, waiting for transfers between devices, outer_step(): lax.psum_scatter(local_slab, 'replica', scatter_dimension=1, tiled=True)  260 us
    reduce_scatter x1, waiting for transfers between devices, inner_pass(): lax.psum_scatter(lax.dot_general(columns, cotangent, (((0,), (0,)), ((),...  186 us
    all_gather x1, waiting for transfers between devices, outer_step(): gathered = lax.all_gather(new_piece, 'replica', axis=1, tiled=True)  49.3 us
  transfers between devices with their start and end apart: 4, of which 3 were waited for; matrix products, arithmetic and copies ran while one was open for 4% of the time, Pallas kernels for 0%

commit v1 on v0

--- a/solution.py
+++ b/solution.py
@@ -18,7 +18,9 @@
     new_piece = (anchor_now - outer_rate * (pseudo_grad + momentum_decay * momentum_new)).astype(
         jnp.bfloat16
     )
-    gathered = lax.all_gather(new_piece, "replica", axis=1, tiled=True)
+    gathered = jnp.concatenate(
+        lax.all_to_all(jnp.stack(lax.axis_size("replica") * [new_piece]), "replica", 0, 0), axis=1
+    )
     return (gathered, momentum_new[:, None])
 
 

time: 542 us -> 509 us (0.939)
  waiting for transfers between devices: 496 us -> 450 us
  starting transfers between devices: 0.17 us -> 11 us
    all_to_all x0 -> x1, waiting for transfers between devices: none -> 160 us  [outer_step(): lax.all_to_all(jnp.stack(lax.axis_size('replica') * [new_piece]), 'replic...]
    reduce_scatter x1, waiting for transfers between devices: 186 us -> 39.4 us  [inner_pass(): lax.psum_scatter(lax.dot_general(columns, cotangent, (((0,), (0,)), ((),...]
    all_gather x1 -> x0, waiting for transfers between devices: 49.3 us -> none  [outer_step(): gathered = lax.all_gather(new_piece, 'replica', axis=1, tiled=True)]
    all_to_all x0 -> x1, starting transfers between devices: none -> 10.9 us  [outer_step(): lax.all_to_all(jnp.stack(lax.axis_size('replica') * [new_piece]), 'replic...]
    reduce_scatter x1, waiting for transfers between devices: 260 us -> 250 us  [outer_step(): lax.psum_scatter(local_slab, 'replica', scatter_dimension=1, tiled=True)]
  transfers between devices with their start and end apart: 4 -> 4, of which waited for: 3 -> 3; matrix products, arithmetic and copies ran while one was open for 4% -> 5% of each run, Pallas kernels for 0% -> 0%
where the time goes in v1:
time: 509 us
  waiting for transfers between devices  450 us (88%)
  matrix products  19 us (4%)
  between operations  15.5 us (3%)
  starting transfers between devices  11 us (2%)
  other arithmetic  7.18 us (1%)
  local copies, waits for them, and re-layouts  6.55 us (1%)
    reduce_scatter x1, waiting for transfers between devices, outer_step(): lax.psum_scatter(local_slab, 'replica', scatter_dimension=1, tiled=True)  250 us
    all_to_all x1, waiting for transfers between devices, outer_step(): lax.all_to_all(jnp.stack(lax.axis_size('replica') * [new_piece]), 'replic...  160 us
    reduce_scatter x1, waiting for transfers between devices, inner_pass(): lax.psum_scatter(lax.dot_general(columns, cotangent, (((0,), (0,)), ((),...  39.4 us
    all_to_all x1, starting transfers between devices, outer_step(): lax.all_to_all(jnp.stack(lax.axis_size('replica') * [new_piece]), 'replic...  10.9 us
  transfers between devices with their start and end apart: 4, of which 3 were waited for; matrix products, arithmetic and copies ran while one was open for 5% of the time, Pallas kernels for 0%

profile of v1, /device:TPU:32, one launch (start us, length us, event | category | flops | bytes accessed | tf_op | source)
XLA Modules:
  0.0 509.0 jit_solution(8265906867997058483)
XLA Ops:
  8.0 0.0 copy-start
  8.0 0.0 reduce-scatter.5.cloned.1.call-start
  8.1 5.5 %bitcast_convert_fusion = f32[2,1024,896]{2,1,0:T(8,128)} fusion(bf16[1,2,1024,896]{3,2,1,0:T(8,128)(2,1)} %param.9), kind=kLoop, calls=%fused_computation.3 | loop fusion | flops 1835008 | bytes 11010048 | tf_op jit(solution)/shard_map/convert_element_type | solution.py:12
  13.5 0.0 reduce-scatter.5.cloned.1.call-update
  13.6 0.0 all-gather.3.cloned.1.call-start
  13.6 0.5 all-gather.3.cloned.1.call-update
  14.1 0.0 reduce-scatter.3.cloned.1.call-start
  14.2 0.0 copy-done
  14.2 9.6 %convolution_convert_fusion = bf16[8192,512]{1,0:T(8,128)(2,1)} fusion(bf16[384,8192]{1,0:T(8,128)(2,1)} %param.6, bf16[384,512]{1,0:T(8,128)(2,1)S(1)} %copy-done), kind=kOutput, calls=%fused_computation | convolution fusion | flops 3225419776 | bytes 15073280 | tf_op jit(solution)/shard_map/dot_general | solution.py:37
  23.8 0.0 copy-start.1
  23.8 0.0 copy-start.2
  23.8 0.0 reduce-scatter.3.cloned.1.call-update
  23.9 250.1 %reduce-scatter.5.cloned.1.call-done = f32[2,32,896]{2,1,0:T(8,128)} async-done(((f32[2,1024,896]{2,1,0:T(8,128)}), f32[2,32,896]{2,1,0:T(8,128)}) %reduce-scatter.5.cloned.1.call-update) | async-done | bytes 229392 | tf_op jit(solution)/shard_map/reduce_scatter | solution.py:13
  274.0 0.0 copy-done.1
  274.0 0.0 copy-done.2
  274.0 1.7 fusion.6
  275.7 2.3 stack.2
  278.0 10.9 %all-to-all-start = ((bf16[32,2,32,896]{3,2,1,0:T(8,128)(2,1)}), bf16[32,2,32,896]{3,2,1,0:T(8,128)(2,1)}, u32[]{:S(2)}, u32[]{:S(2)}) async-start(bf16[32,2,32,896]{3,2,1,0:T(8,128)(2,1)} %stack.2), calls=%async_computation.2 | async-start | bytes 7340032 | tf_op jit(solution)/shard_map/all_to_all | solution.py:22
  288.9 0.0 all-gather.3.cloned.1.call-done
  288.9 9.4 %fusion.2 = bf16[384,512]{1,0:T(8,128)(2,1)} fusion(bf16[384,8192]{1,0:T(8,128)(2,1)} %param.6, bf16[1,8192,512]{2,1,0:T(8,128)(2,1)} %all-gather.3.cloned.1.call-done), kind=kOutput, calls=%fused_computation.4 | convolution fusion | flops 3221422080 | bytes 15073280 | tf_op jit(solution)/shard_map/dot_general | solution.py:30
  298.3 159.7 %all-to-all-done = bf16[32,2,32,896]{3,2,1,0:T(8,128)(2,1)} async-done(((bf16[32,2,32,896]{3,2,1,0:T(8,128)(2,1)}), bf16[32,2,32,896]{3,2,1,0:T(8,128)(2,1)}, u32[]{:S(2)}, u32[]{:S(2)}) %all-to-all-start) | async-done | bytes 3670048 | tf_op jit(solution)/shard_map/all_to_all | solution.py:22
  458.0 4.2 copy.16
  462.2 39.4 %reduce-scatter.3.cloned.1.call-done = bf16[1024,512]{1,0:T(8,128)(2,1)} async-done(((bf16[8192,512]{1,0:T(8,128)(2,1)}), bf16[1024,512]{1,0:T(8,128)(2,1)}) %reduce-scatter.3.cloned.1.call-update) | async-done | bytes 1048592 | tf_op jit(solution)/shard_map/reduce_scatter | solution.py:36
Async XLA Ops:
  8.0 6.2 %copy-start = (bf16[384,512]{1,0:T(8,128)(2,1)S(1)}, bf16[384,512]{1,0:T(8,128)(2,1)}, u32[]{:S(2)}) copy-start(bf16[384,512]{1,0:T(8,128)(2,1)} %param.8) | copy-start | bytes 1179652
  8.0 266.0 %reduce-scatter.5.cloned.1.call-start = ((), (), s32[]{:S(2)}) async-start(), calls=%async_computation.4 | async-start | bytes 7569408 | tf_op jit(solution)/shard_map/reduce_scatter | solution.py:13
  13.6 275.3 %all-gather.3.cloned.1.call-start = ((), (), s32[]{:S(2)}) async-start(), calls=%async_computation.5 | async-start | bytes 9437184 | tf_op jit(solution)/shard_map/all_gather | solution.py:32
  14.1 487.4 %reduce-scatter.3.cloned.1.call-start = ((), (), s32[]{:S(2)}) async-start(), calls=%async_computation.3 | async-start | bytes 9437184 | tf_op jit(solution)/shard_map/reduce_scatter | solution.py:36
  23.8 250.1 %copy-start.1 = (f32[2,1,32,896]{3,2,1,0:T(8,128)S(1)}, f32[2,1,32,896]{3,2,1,0:T(8,128)}, u32[]{:S(2)}) copy-start(f32[2,1,32,896]{3,2,1,0:T(8,128)} %param.11) | copy-start | bytes 688132
  23.8 250.1 %copy-start.2 = (bf16[2,1,32,896]{3,2,1,0:T(8,128)(2,1)S(1)}, bf16[2,1,32,896]{3,2,1,0:T(8,128)(2,1)}, u32[]{:S(2)}) copy-start(bf16[2,1,32,896]{3,2,1,0:T(8,128)(2,1)} %param.10) | copy-start | bytes 344068
  278.0 180.0 %all-to-all-start = ((bf16[32,2,32,896]{3,2,1,0:T(8,128)(2,1)}), bf16[32,2,32,896]{3,2,1,0:T(8,128)(2,1)}, u32[]{:S(2)}, u32[]{:S(2)}) async-start(bf16[32,2,32,896]{3,2,1,0:T(8,128)(2,1)} %stack.2), calls=%async_computation.2 | async-start | bytes 7340032 | tf_op jit(solution)/shard_map/all_to_all | solution.py:22
Sparse Core Ops, SparseCore 0:
  13.7 260.2 reduce-scatter.4
  278.7 222.8 reduce-scatter.2
Sparse Core Ops, SparseCore 1:
  16.7 178.4 all-gather.2
